TPU v7x, 512 devices: a whole 4x4x16 slice. The times are simulated.
512 devices in a mesh: layer: 4 (over y_hi, core), feat: 128 (over y_lo, z, x).
Axes of the slice: x: 4, y: 4 (y_hi: 2, y_lo: 2; y = y_hi * 2 + y_lo), z: 16, core: 2. Of those that a mesh axis runs over, the one named last changes fastest.
Arguments:
- resid_stream: bfloat16 [128, 4, 2304], P('feat', 'layer'), may hold values from -6 to 6
- enc_mantissa: bfloat16 [4, 2304, 16384], P('layer', None, 'feat'), may hold values from -96 to 96
- enc_exponent: int32 [4, 18, 128], P('layer', None, 'feat'), may hold values from -11 to -10
- enc_bias: float32 [4, 16384], P('layer', 'feat'), may hold values from -3 to 3
- dec_weight: bfloat16 [10, 16384, 2304], P(None, 'feat', 'layer'), may hold values from -0.046875 to 0.046875
- dec_bias: float32 [4, 2304], P('layer'), may hold values from -3 to 3
Outputs:
- recon: bfloat16 [128, 4, 2304], P('feat', 'layer')
All inputs are finite; a program needn't handle non-finite values.
Results may differ from a plain program's by a relative error of at most 0.0044.
Values may be sent and summed in bfloat16 or wider, within the bound.
A program may use at most 64 MiB of HBM per device.

v0:
```python
import jax
import jax.numpy as jnp
from jax import lax
from jax.sharding import PartitionSpec as P

BLK = 128


def shards(resid_stream, enc_mantissa, enc_exponent, enc_bias, dec_weight, dec_bias):
    layer_count = lax.axis_size("layer")
    width = resid_stream.shape[2]
    feat_local = enc_mantissa.shape[2]
    scales = jnp.exp2(enc_exponent[0].astype(jnp.float32))
    blocks = enc_mantissa[0].astype(jnp.float32).reshape(width // BLK, BLK, feat_local // BLK, BLK)
    weight = (blocks * scales[:, None, :, None]).reshape(width, feat_local).astype(jnp.bfloat16)
    bias_row = enc_bias[0][None, :]
    pre_act = jnp.dot(
        lax.all_gather(resid_stream, "feat", axis=0, tiled=True)[:, 0, :],
        weight,
        preferred_element_type=jnp.float32,
    )
    latent = jnp.maximum(pre_act + bias_row, 0.0).astype(jnp.bfloat16)
    stacked = lax.all_gather(latent[None], "layer", axis=0, tiled=True)
    group_index = lax.axis_index("layer")
    first_pair = group_index * (group_index + 1) // 2
    decoders = lax.all_gather(dec_weight, "layer", axis=2, tiled=True)
    chosen = lax.dynamic_slice_in_dim(decoders, first_pair, layer_count, 0)
    active = jnp.arange(layer_count, dtype=jnp.int32) <= group_index
    masked = jnp.where(active[:, None, None], stacked, jnp.zeros_like(stacked))
    summed = lax.psum_scatter(
        jnp.einsum("lnf,lfd->nd", masked, chosen, preferred_element_type=jnp.float32),
        "feat",
        scatter_dimension=0,
        tiled=True,
    )
    return (summed + dec_bias[0][None, :]).astype(jnp.bfloat16)[:, None, :]


def solution(mesh):
    in_specs = (
        P("feat", "layer", None),
        P("layer", None, "feat"),
        P("layer", None, "feat"),
        P("layer", "feat"),
        P(None, "feat", "layer"),
        P("layer", None),
    )
    out_specs = P("feat", "layer", None)
    return jax.shard_map(shards, mesh=mesh, in_specs=in_specs, out_specs=out_specs, check_vma=False)
```

profile of v0, /device:TPU:24, one launch (start us, length us, event | category | flops | bytes accessed | tf_op | source)
XLA Modules:
  0.0 1456.7 jit_solution(15859345286378986823)
XLA Ops:
  6.5 0.0 copy-start.3
  6.5 0.0 copy-start.1
  6.5 0.0 copy-start.4
  6.5 0.0 copy-start.2
  6.5 0.0 all-gather.3.cloned.1.call-start
  6.6 0.7 all-gather.3.cloned.1.call-update
  7.3 0.0 all-reduce.3.cloned.1.call-start
  7.3 0.0 copy-done.3
  7.4 0.1 broadcast_bitcast_fusion
  7.4 0.0 copy-done.1
  7.4 317.7 %all_gather.9 = bf16[128,1,2304]{2,1,0:T(2,128)(2,1)S(1)} all-gather(bf16[1,1,2304]{2,1,0:T(2,128)(2,1)S(1)} %copy-done.1), channel_id=1, replica_groups=mesh['layer'=4,'feat'=128] {'feat'}, dimensions={0}, use_global_device_ids=true | all-gather | bytes 594432 | tf_op jit(solution)/shard_map/all_gather | solution.py:18
  325.1 0.0 copy-done.4
  325.1 0.0 copy-done.2
  325.1 0.8 fusion.3
  325.9 7.0 all-gather
  332.9 0.1 copy.14
  333.0 0.0 all-gather.3.cloned.1.call-done
  333.0 3.6 convolution_bitcast_fusion
  336.6 0.0 copy-start
  336.6 0.0 all-reduce.3.cloned.1.call-update
  336.7 1.3 dynamic-slice
  337.9 1109.8 %all-reduce.3.cloned.1.call-done = f32[128,2304]{1,0:T(8,128)} async-done(((f32[128,2304]{1,0:T(8,128)}), f32[128,2304]{1,0:T(8,128)}) %all-reduce.3.cloned.1.call-update) | async-done | bytes 1179664
  1447.7 0.0 copy-done
  1447.7 2.1 fusion.13
  (2 shorter events, 0.0 us)
Async XLA Ops:
  6.5 0.8 copy-start.3
  6.5 0.9 copy-start.1
  6.5 318.6 %copy-start.4 = (f32[1,128]{1,0:T(1,128)S(1)}, f32[1,128]{1,0:T(1,128)}, u32[]{:S(2)}) copy-start(f32[1,128]{1,0:T(1,128)} %param.9) | copy-start | bytes 1540
  6.5 318.6 %copy-start.2 = (bf16[1,2304,128]{2,1,0:T(8,128)(2,1)S(1)}, bf16[1,2304,128]{2,1,0:T(8,128)(2,1)}, u32[]{:S(2)}) copy-start(bf16[1,2304,128]{2,1,0:T(8,128)(2,1)} %param.7) | copy-start | bytes 1769476
  6.5 326.5 %all-gather.3.cloned.1.call-start = ((), (), s32[]{:S(2)}) async-start(), calls=%async_computation | async-start | bytes 7372800 | tf_op jit(solution)/shard_map/all_gather | solution.py:26
  7.3 1440.4 %all-reduce.3.cloned.1.call-start = ((), (), s32[]{:S(2)}) async-start(), calls=%async_computation.1 | async-start | bytes 2359296
  336.6 1111.1 %copy-start = (f32[1,2304]{1,0:T(1,128)S(1)}, f32[1,2304]{1,0:T(1,128)}, u32[]{:S(2)}) copy-start(f32[1,2304]{1,0:T(1,128)} %param.11) | copy-start | bytes 27652
Sparse Core Ops, SparseCore 0:
  9.5 59.8 all-gather.2
  336.8 1110.8 all-reduce.2
where the time goes:
time: 1460 us
  waiting for transfers between devices  1110 us (76%)
  blocking collectives  325 us (22%)
    unnamed x3, waiting for transfers between devices  1110 us
    all_gather x1, blocking collectives, shards(): lax.all_gather(resid_stream, 'feat', axis=0, tiled=True)[:, 0, :]  318 us
  transfers between devices with their start and end apart: 2, of which 1 were waited for; matrix products, arithmetic and copies ran while one was open for 0% of the time, Pallas kernels for 0%

commit v1 on v0

v1 whole, which is shorter than its diff:
```python
import jax
import jax.numpy as jnp
from jax import lax
from jax.experimental import pallas as pl
from jax.experimental.pallas import tpu as pltpu
from jax.sharding import PartitionSpec as P

LY = 4
NX = 4
NP = 8
NZ = 16
BLK = 128
PITCH = 24
MESH = pl.DeviceIdType.MESH


def pow2(exponent):
    down = -exponent
    scale = jnp.ones(exponent.shape, jnp.float32)
    for bit in range(7):
        scale = scale * jnp.where((down & (1 << bit)) != 0, jnp.float32(2.0 ** -(1 << bit)), jnp.float32(1.0))
    return scale


def kernel(
    x_ref, m_ref, e_ref, eb_ref, d_ref, db_ref, out_ref,
    w_v, d_v, own, rows, stage, xg, lat, part, rs1, stage2, sb, rz,
    loc_sem, zs, zr, ps, pr, ls, lr, rs_s, rs_r, fs, fr,
):
    layer = lax.axis_index("layer")
    feat = lax.axis_index("feat")
    y_lo = feat // (NZ * NX)
    z = (feat // NX) % NZ
    x = feat % NX
    p = y_lo * NX + x
    width = x_ref.shape[1]
    blocks = width // BLK
    cols = d_ref.shape[1]
    chunks = part.shape[3] // BLK

    def feat_of(place, zz):
        return (place // NX) * (NZ * NX) + zz * NX + place % NX

    load_w = pltpu.make_async_copy(m_ref, w_v, loc_sem.at[0])
    load_d = pltpu.make_async_copy(d_ref, d_v, loc_sem.at[1])
    load_w.start()
    load_d.start()

    barrier = pltpu.get_barrier_semaphore()

    @pl.loop(1, NZ)
    def _(k):
        pl.semaphore_signal(barrier, inc=1, device_id=(layer, feat_of(p, (z + k) % NZ)), device_id_type=MESH)

    @pl.loop(1, LY * NP)
    def _(k):
        q = (layer * NP + p + k) % (LY * NP)
        pl.semaphore_signal(barrier, inc=1, device_id=(q // NP, feat_of(q % NP, z)), device_id_type=MESH)

    for b in range(blocks):
        own[b : b + 1, :] = x_ref[0:1, b * BLK : (b + 1) * BLK].astype(jnp.float32)
    rows[z] = own[0:blocks, :].astype(jnp.bfloat16)
    for t in range(LY):
        part[t, :, :, 512:640] = jnp.zeros((NP, NZ, 128), jnp.bfloat16)

    pl.semaphore_wait(barrier, (NZ - 1) + (LY * NP - 1))

    def z_copy(slot, other):
        return pltpu.make_async_remote_copy(
            src_ref=rows.at[z], dst_ref=rows.at[slot], send_sem=zs.at[other], recv_sem=zr.at[slot],
            device_id=(layer, feat_of(p, other)), device_id_type=MESH,
        )

    @pl.loop(1, NZ)
    def _(k):
        z_copy(z, (z + k) % NZ).start()

    load_w.wait()
    scales = pow2(e_ref[0:1, :])
    for b in range(blocks):
        piece = slice(b * BLK, (b + 1) * BLK)
        w_v[piece, :] = (w_v[piece, :].astype(jnp.float32) * scales[0:1, b : b + 1]).astype(jnp.bfloat16)

    @pl.loop(1, NZ)
    def _(k):
        other = (z + k) % NZ
        z_copy(other, other).wait_recv()

    for zz in range(NZ):
        stage[zz * PITCH : zz * PITCH + blocks, :] = rows[zz].astype(jnp.float32)
    for b in range(blocks):
        xg[p, :, b * BLK : (b + 1) * BLK] = stage[pl.ds(b, NZ, stride=PITCH), :].astype(jnp.bfloat16)

    def p_copy(slot, other):
        return pltpu.make_async_remote_copy(
            src_ref=xg.at[p], dst_ref=xg.at[slot], send_sem=ps.at[other], recv_sem=pr.at[slot],
            device_id=(layer, feat_of(other, z)), device_id_type=MESH,
        )

    @pl.loop(1, NP)
    def _(k):
        p_copy(p, (p + k) % NP).start()

    @pl.loop(1, NP)
    def _(k):
        other = (p + k) % NP
        p_copy(other, other).wait_recv()

    tokens = NP * NZ
    pre = jnp.dot(xg[...].reshape(tokens, width), w_v[...], preferred_element_type=jnp.float32)
    lat[layer] = jnp.maximum(pre + eb_ref[...], 0.0).astype(jnp.bfloat16)

    def l_copy(slot, other):
        return pltpu.make_async_remote_copy(
            src_ref=lat.at[layer], dst_ref=lat.at[slot], send_sem=ls.at[other], recv_sem=lr.at[slot],
            device_id=(other, feat), device_id_type=MESH,
        )

    @pl.loop(1, LY)
    def _(k):
        l_copy(layer, (layer + k) % LY).start()

    load_d.wait()

    @pl.loop(1, LY)
    def _(k):
        other = (layer + k) % LY
        l_copy(other, other).wait_recv()

    for t in range(LY):
        total = jnp.zeros((tokens, cols), jnp.float32)
        for s in range(t + 1):
            total = total + lax.dot_general(
                lat[s], d_v[t * (t + 1) // 2 + s], (((1,), (1,)), ((), ())), preferred_element_type=jnp.float32
            )
        part[t, :, :, 0:cols] = total.reshape(NP, NZ, cols).astype(jnp.bfloat16)

    def r_copy(src, slot, other):
        return pltpu.make_async_remote_copy(
            src_ref=part.at[src // NP, src % NP], dst_ref=rs1.at[slot // NP, slot % NP],
            send_sem=rs_s.at[other], recv_sem=rs_r.at[slot],
            device_id=(other // NP, feat_of(other % NP, z)), device_id_type=MESH,
        )

    mine = layer * NP + p

    @pl.loop(1, LY * NP)
    def _(k):
        q = (mine + k) % (LY * NP)
        r_copy(q, mine, q).start()

    rs1[layer, p] = part[layer, p]

    @pl.loop(1, LY * NP)
    def _(k):
        q = (mine + k) % (LY * NP)
        r_copy(q, q, q).wait_recv()

    for s in range(LY):
        total = rs1[s, 0].astype(jnp.float32)
        for place in range(1, NP):
            total = total + rs1[s, place].astype(jnp.float32)
        for c in range(chunks):
            stage2[pl.ds(s * chunks + c, NZ, stride=PITCH), :] = total[:, c * BLK : (c + 1) * BLK]
    for zz in range(NZ):
        sb[zz] = stage2[zz * PITCH : zz * PITCH + LY * chunks, :].astype(jnp.bfloat16)

    def f_copy(slot, other):
        return pltpu.make_async_remote_copy(
            src_ref=sb.at[other], dst_ref=rz.at[slot], send_sem=fs.at[other], recv_sem=fr.at[slot],
            device_id=(layer, feat_of(p, other)), device_id_type=MESH,
        )

    @pl.loop(1, NZ)
    def _(k):
        f_copy(z, (z + k) % NZ).start()

    rz[z] = sb[z]

    @pl.loop(1, NZ)
    def _(k):
        other = (z + k) % NZ
        f_copy(other, other).wait_recv()

    total = rz[0].astype(jnp.float32)
    for zz in range(1, NZ):
        total = total + rz[zz].astype(jnp.float32)

    half = BLK // 2
    low = lax.broadcasted_iota(jnp.int32, (1, BLK), 1) < half
    turned = pltpu.roll(total, half, 1)
    at = 0
    for pair in range(LY // 2):
        even, odd = pair * 2 * chunks, (pair * 2 + 1) * chunks
        pieces = [total[even + c : even + c + 1, :] for c in range(chunks - 1)]
        pieces.append(jnp.where(low, total[even + chunks - 1 : even + chunks, :], turned[odd : odd + 1, :]))
        for c in range(1, chunks):
            pieces.append(jnp.where(low, turned[odd + c - 1 : odd + c, :], turned[odd + c : odd + c + 1, :]))
        for piece in pieces:
            out_ref[0:1, at : at + BLK] = (piece + db_ref[0:1, at : at + BLK]).astype(jnp.bfloat16)
            at += BLK

    @pl.loop(1, NZ)
    def _(k):
        other = (z + k) % NZ
        z_copy(z, other).wait_send()
        f_copy(z, other).wait_send()

    @pl.loop(1, NP)
    def _(k):
        p_copy(p, (p + k) % NP).wait_send()

    @pl.loop(1, LY)
    def _(k):
        l_copy(layer, (layer + k) % LY).wait_send()

    @pl.loop(1, LY * NP)
    def _(k):
        q = (mine + k) % (LY * NP)
        r_copy(q, mine, q).wait_send()


def shards(resid_stream, enc_mantissa, enc_exponent, enc_bias, dec_weight, dec_bias):
    width = resid_stream.shape[2]
    feats = enc_mantissa.shape[2]
    pairs, _, cols = dec_weight.shape
    blocks = width // BLK
    padded = (cols + BLK - 1) // BLK * BLK
    vm = pl.BlockSpec(memory_space=pltpu.VMEM)
    hbm = pl.BlockSpec(memory_space=pl.ANY)
    dma = pltpu.SemaphoreType.DMA
    bf, f32 = jnp.bfloat16, jnp.float32
    out = pl.pallas_call(
        kernel,
        out_shape=jax.ShapeDtypeStruct((1, width), bf),
        in_specs=[vm, hbm, vm, vm, hbm, vm],
        out_specs=vm,
        scratch_shapes=[
            pltpu.VMEM((width, feats), bf),
            pltpu.VMEM((pairs, cols, feats), bf),
            pltpu.VMEM((PITCH, BLK), f32),
            pltpu.VMEM((NZ, blocks, BLK), bf),
            pltpu.VMEM((NZ * PITCH, BLK), f32),
            pltpu.VMEM((NP, NZ, width), bf),
            pltpu.VMEM((LY, NP * NZ, feats), bf),
            pltpu.VMEM((LY, NP, NZ, padded), bf),
            pltpu.VMEM((LY, NP, NZ, padded), bf),
            pltpu.VMEM((NZ * PITCH, BLK), f32),
            pltpu.VMEM((NZ, LY * padded // BLK, BLK), bf),
            pltpu.VMEM((NZ, LY * padded // BLK, BLK), bf),
            dma((2,)),
            dma((NZ,)), dma((NZ,)),
            dma((NP,)), dma((NP,)),
            dma((LY,)), dma((LY,)),
            dma((LY * NP,)), dma((LY * NP,)),
            dma((NZ,)), dma((NZ,)),
        ],
        compiler_params=pltpu.CompilerParams(collective_id=0, has_side_effects=True),
    )(
        resid_stream.reshape(1, width),
        enc_mantissa[0],
        enc_exponent.reshape(1, blocks),
        enc_bias,
        dec_weight.transpose(0, 2, 1),
        dec_bias,
    )
    return out[:, None, :]


def solution(mesh):
    in_specs = (
        P("feat", "layer", None),
        P("layer", None, "feat"),
        P("layer", None, "feat"),
        P("layer", "feat"),
        P(None, "feat", "layer"),
        P("layer", None),
    )
    out_specs = P("feat", "layer", None)
    return jax.shard_map(shards, mesh=mesh, in_specs=in_specs, out_specs=out_specs, check_vma=False)
```

time: 1460 us -> 65.2 us (0.04)
  the two profiles are of different devices: /device:TPU:24 before, /device:TPU:1 now
where the time goes in v1:
time: 65.2 us; the launch traced here: 65 us
  Pallas kernels  63.7 us (98%)
  local copies, waits for them, and re-layouts  1.31 us (2%)
    pallas_call x1, Pallas kernels, shards(): pl.pallas_call(kernel, out_shape=jax.ShapeDtypeStruct((1, width), bf), in...  63.7 us
    unnamed x1, local copies, waits for them, and re-layouts  1.31 us

profile of v1, /device:TPU:1, one launch (start us, length us, event | category | flops | bytes accessed | tf_op | source)
XLA Modules:
  0.0 65.0 jit_solution(3827438886290220333)
XLA Ops:
  0.0 63.7 %shard_map.64 = bf16[1,2304]{1,0:T(2,128)(2,1)} custom-call(bf16[1,2304]{1,0:T(2,128)(2,1)} %bitcast.8, bf16[2304,128]{1,0:T(8,128)(2,1)} %bitcast.6, s32[1,18]{1,0:T(1,128)} %bitcast.9, f32[1,128]{1,0:T(1,128)} %eb_ref.1, bf16[10,576,128]{2,1,0:T(8,128)(2,1)} %bitcast.5, f32[1,2304]{1,0:T(1,128)} %db_ref.1), custom_call_target="tpu_custom_call" | custom-call | tf_op jit(solution)/shard_map/pallas_call | solution.py:233
  63.7 1.3 %copy.8 = bf16[1,1,2304]{2,1,0:T(2,128)(2,1)} copy(bf16[1,1,2304]{2,1,0:T(2,128)(2,1)} %bitcast.7) | data formatting | bytes 9216

commit v2 on v1

--- a/solution.py
+++ b/solution.py
@@ -12,6 +12,8 @@
 BLK = 128
 PITCH = 24
 MESH = pl.DeviceIdType.MESH
+RING = (2, 1, 3, 0)
+PLANE = sorted(((dy, dx) for dy in RING for dx in RING), key=lambda s: -(min(s[0], 4 - s[0]) + min(s[1], 4 - s[1])))
 
 
 def pow2(exponent):
@@ -41,6 +43,14 @@
     def feat_of(place, zz):
         return (place // NX) * (NZ * NX) + zz * NX + place % NX
 
+    def far_first(send):
+        send((z + NZ // 2) % NZ)
+
+        @pl.loop(1, NZ // 2)
+        def _(k):
+            send((z + NZ // 2 - k) % NZ)
+            send((z + NZ // 2 + k) % NZ)
+
     load_w = pltpu.make_async_copy(m_ref, w_v, loc_sem.at[0])
     load_d = pltpu.make_async_copy(d_ref, d_v, loc_sem.at[1])
     load_w.start()
@@ -71,9 +81,7 @@
             device_id=(layer, feat_of(p, other)), device_id_type=MESH,
         )
 
-    @pl.loop(1, NZ)
-    def _(k):
-        z_copy(z, (z + k) % NZ).start()
+    far_first(lambda other: z_copy(z, other).start())
 
     load_w.wait()
     scales = pow2(e_ref[0:1, :])
@@ -97,9 +105,10 @@
             device_id=(layer, feat_of(other, z)), device_id_type=MESH,
         )
 
-    @pl.loop(1, NP)
-    def _(k):
-        p_copy(p, (p + k) % NP).start()
+    for dy in (1, 0):
+        for dx in RING:
+            if dy or dx:
+                p_copy(p, (y_lo + dy) % 2 * NX + (x + dx) % NX).start()
 
     @pl.loop(1, NP)
     def _(k):
@@ -144,10 +153,13 @@
 
     mine = layer * NP + p
 
-    @pl.loop(1, LY * NP)
-    def _(k):
-        q = (mine + k) % (LY * NP)
-        r_copy(q, mine, q).start()
+    y, core = layer // 2 * 2 + y_lo, layer % 2
+    for dy, dx in PLANE:
+        for dc in (1, 0):
+            if dy or dx or dc:
+                to_y = (y + dy) % 4
+                to = (to_y // 2 * 2 + (core + dc) % 2) * NP + to_y % 2 * NX + (x + dx) % NX
+                r_copy(to, mine, to).start()
 
     rs1[layer, p] = part[layer, p]
 
@@ -171,9 +183,7 @@
             device_id=(layer, feat_of(p, other)), device_id_type=MESH,
         )
 
-    @pl.loop(1, NZ)
-    def _(k):
-        f_copy(z, (z + k) % NZ).start()
+    far_first(lambda other: f_copy(z, other).start())
 
     rz[z] = sb[z]
 

time: 65.2 us -> 59.3 us (0.910)
  Pallas kernels: 63.7 us -> 57.8 us
    pallas_call x1, Pallas kernels: 63.7 us -> 57.8 us  [shards(): pl.pallas_call(kernel, out_shape=jax.ShapeDtypeStruct((1, width), bf), in...]
where the time goes in v2:
time: 59.3 us; the launch traced here: 59.1 us
  Pallas kernels  57.8 us (97%)
  local copies, waits for them, and re-layouts  1.31 us (2%)
    pallas_call x1, Pallas kernels, shards(): pl.pallas_call(kernel, out_shape=jax.ShapeDtypeStruct((1, width), bf), in...  57.8 us
    unnamed x1, local copies, waits for them, and re-layouts  1.31 us

profile of v2, /device:TPU:1, one launch (start us, length us, event | category | flops | bytes accessed | tf_op | source)
XLA Modules:
  0.0 59.1 jit_solution(11333903788409541468)
XLA Ops:
  0.0 57.8 %shard_map.64 = bf16[1,2304]{1,0:T(2,128)(2,1)} custom-call(bf16[1,2304]{1,0:T(2,128)(2,1)} %bitcast.8, bf16[2304,128]{1,0:T(8,128)(2,1)} %bitcast.6, s32[1,18]{1,0:T(1,128)} %bitcast.9, f32[1,128]{1,0:T(1,128)} %eb_ref.1, bf16[10,576,128]{2,1,0:T(8,128)(2,1)} %bitcast.5, f32[1,2304]{1,0:T(1,128)} %db_ref.1), custom_call_target="tpu_custom_call" | custom-call | tf_op jit(solution)/shard_map/pallas_call | solution.py:243
  57.8 1.3 %copy.8 = bf16[1,1,2304]{2,1,0:T(2,128)(2,1)} copy(bf16[1,1,2304]{2,1,0:T(2,128)(2,1)} %bitcast.7) | data formatting | bytes 9216

commit v3 on v1

v3 whole, which is shorter than its diff:
```python
import jax
import jax.numpy as jnp
from jax import lax
from jax.experimental import pallas as pl
from jax.experimental.pallas import tpu as pltpu
from jax.sharding import PartitionSpec as P

LY = 4
NX = 4
NP = 8
NZ = 16
BLK = 128
PITCH = 24
MESH = pl.DeviceIdType.MESH
GROUP = 8
REACH = 4
Z_STEPS = (-4, 4, -3, 3, -2, 2, -1, 1)
PASSED = (-1, 1, -2, 2, -3, 3, -4)
RING = (2, 1, 3, 0)
PLANE = sorted(
    ((dy, dx, dc) for dy in RING for dx in RING for dc in (1, 0) if dy or dx or dc),
    key=lambda s: -(min(s[0], 4 - s[0]) + min(s[1], 4 - s[1])),
)


def pow2(exponent):
    down = -exponent
    scale = jnp.ones(exponent.shape, jnp.float32)
    for bit in range(7):
        scale = scale * jnp.where((down & (1 << bit)) != 0, jnp.float32(2.0 ** -(1 << bit)), jnp.float32(1.0))
    return scale


def kernel(
    x_ref, m_ref, e_ref, eb_ref, d_ref, db_ref, out_ref,
    w_v, d_v, own, rows, stage, xg, lat, part, rs1, stage2, sb, rz,
    loc_sem, zs, zf, zr, ps, pr, ls, lr, rs_s, rs_r, fs, fr,
):
    layer = lax.axis_index("layer")
    feat = lax.axis_index("feat")
    y_lo = feat // (NZ * NX)
    z = (feat // NX) % NZ
    x = feat % NX
    p = y_lo * NX + x
    y, core = layer // 2 * 2 + y_lo, layer % 2
    mine = layer * NP + p
    width = x_ref.shape[1]
    blocks = width // BLK
    cols = d_ref.shape[1]
    chunks = part.shape[4] // BLK

    def feat_of(place, zz):
        return (place // NX) * (NZ * NX) + zz * NX + place % NX

    def along(step):
        return (z + step + NZ) % NZ

    def row_of(group, i):
        return (z + NZ - REACH + GROUP * group + i) % NZ

    def plane_to(dy, dx, dc):
        to_y = (y + dy) % 4
        return (to_y // 2 * 2 + (core + dc) % 2) * NP + to_y % 2 * NX + (x + dx) % NX

    load_w = pltpu.make_async_copy(m_ref, w_v, loc_sem.at[0])
    load_d = pltpu.make_async_copy(d_ref, d_v, loc_sem.at[1])
    load_w.start()
    load_d.start()

    barrier = pltpu.get_barrier_semaphore()
    for step in Z_STEPS:
        pl.semaphore_signal(barrier, inc=1, device_id=(layer, feat_of(p, along(step))), device_id_type=MESH)
    for dy, dx, dc in PLANE:
        to = plane_to(dy, dx, dc)
        pl.semaphore_signal(barrier, inc=1, device_id=(to // NP, feat_of(to % NP, z)), device_id_type=MESH)

    for b in range(blocks):
        own[b : b + 1, :] = x_ref[0:1, b * BLK : (b + 1) * BLK].astype(jnp.float32)
    rows[z] = own[0:blocks, :].astype(jnp.bfloat16)
    for g in range(2):
        for t in range(LY):
            part[g, t, :, :, 512:640] = jnp.zeros((NP, GROUP, 128), jnp.bfloat16)

    pl.semaphore_wait(barrier, len(Z_STEPS) + len(PLANE))

    def z_copy(row, sems, sem, step):
        return pltpu.make_async_remote_copy(
            src_ref=rows.at[row], dst_ref=rows.at[row], send_sem=sems.at[sem], recv_sem=zr.at[row],
            device_id=(layer, feat_of(p, along(step))), device_id_type=MESH,
        )

    for n, step in enumerate(Z_STEPS):
        z_copy(z, zs, n, step).start()

    load_w.wait()
    scales = pow2(e_ref[0:1, :])
    for b in range(blocks):
        piece = slice(b * BLK, (b + 1) * BLK)
        w_v[piece, :] = (w_v[piece, :].astype(jnp.float32) * scales[0:1, b : b + 1]).astype(jnp.bfloat16)

    def arrived(step):
        z_copy(along(step), zs, 0, 1).wait_recv()

    for n, step in enumerate(PASSED):
        arrived(step)
        z_copy(along(step), zf, n, REACH if step < 0 else -REACH).start()

    def p_copy(group, slot, other):
        return pltpu.make_async_remote_copy(
            src_ref=xg.at[group, p], dst_ref=xg.at[group, slot],
            send_sem=ps.at[group, other], recv_sem=pr.at[group, slot],
            device_id=(layer, feat_of(other, z)), device_id_type=MESH,
        )

    def spread(g):
        for i in range(GROUP):
            stage[i * PITCH : i * PITCH + blocks, :] = rows[row_of(g, i)].astype(jnp.float32)
        for b in range(blocks):
            xg[g, p, :, b * BLK : (b + 1) * BLK] = stage[pl.ds(b, GROUP, stride=PITCH), :].astype(jnp.bfloat16)
        for dy in (1, 0):
            for dx in RING:
                if dy or dx:
                    p_copy(g, p, (y_lo + dy) % 2 * NX + (x + dx) % NX).start()

    spread(0)
    for step in range(REACH, REACH + GROUP):
        arrived(step)
    spread(1)

    def l_copy(group, slot, other):
        return pltpu.make_async_remote_copy(
            src_ref=lat.at[layer, group], dst_ref=lat.at[slot, group],
            send_sem=ls.at[group, other], recv_sem=lr.at[group, slot],
            device_id=(other, feat), device_id_type=MESH,
        )

    tokens = NP * GROUP

    def encode(g):
        @pl.loop(1, NP)
        def _(k):
            other = (p + k) % NP
            p_copy(g, other, other).wait_recv()

        pre = jnp.dot(xg[g].reshape(tokens, width), w_v[...], preferred_element_type=jnp.float32)
        lat[layer, g] = jnp.maximum(pre + eb_ref[...], 0.0).astype(jnp.bfloat16)
        for k in (2, 3, 1):
            l_copy(g, layer, (layer + k) % LY).start()

    def r_copy(group, src, slot, other):
        return pltpu.make_async_remote_copy(
            src_ref=part.at[group, src // NP, src % NP], dst_ref=rs1.at[group, slot // NP, slot % NP],
            send_sem=rs_s.at[group, other], recv_sem=rs_r.at[group, slot],
            device_id=(other // NP, feat_of(other % NP, z)), device_id_type=MESH,
        )

    def decode(g):
        @pl.loop(1, LY)
        def _(k):
            other = (layer + k) % LY
            l_copy(g, other, other).wait_recv()

        for t in range(LY):
            total = jnp.zeros((tokens, cols), jnp.float32)
            for s in range(t + 1):
                total = total + lax.dot_general(
                    lat[s, g], d_v[t * (t + 1) // 2 + s], (((1,), (1,)), ((), ())),
                    preferred_element_type=jnp.float32,
                )
            part[g, t, :, :, 0:cols] = total.reshape(NP, GROUP, cols).astype(jnp.bfloat16)
        for dy, dx, dc in PLANE:
            to = plane_to(dy, dx, dc)
            r_copy(g, to, mine, to).start()
        rs1[g, layer, p] = part[g, layer, p]

    encode(0)
    load_d.wait()
    decode(0)
    encode(1)
    decode(1)

    def f_copy(row, slot):
        return pltpu.make_async_remote_copy(
            src_ref=sb.at[row], dst_ref=rz.at[slot], send_sem=fs.at[row], recv_sem=fr.at[slot],
            device_id=(layer, feat_of(p, row)), device_id_type=MESH,
        )

    def gathered(g):
        @pl.loop(1, LY * NP)
        def _(k):
            q = (mine + k) % (LY * NP)
            r_copy(g, q, q, q).wait_recv()

        for s in range(LY):
            total = rs1[g, s, 0].astype(jnp.float32)
            for place in range(1, NP):
                total = total + rs1[g, s, place].astype(jnp.float32)
            for c in range(chunks):
                stage2[pl.ds(s * chunks + c, GROUP, stride=PITCH), :] = total[:, c * BLK : (c + 1) * BLK]
        for i in range(GROUP):
            sb[row_of(g, i)] = stage2[i * PITCH : i * PITCH + LY * chunks, :].astype(jnp.bfloat16)

    gathered(0)
    for step in (-4, 3, -3, 2, -2, 1, -1):
        f_copy(along(step), z).start()
    rz[z] = sb[z]
    gathered(1)
    for step in (8, 7, 9, 6, 10, 5, 11, 4):
        f_copy(along(step), z).start()

    @pl.loop(1, NZ)
    def _(k):
        other = (z + k) % NZ
        f_copy(other, other).wait_recv()

    total = rz[0].astype(jnp.float32)
    for zz in range(1, NZ):
        total = total + rz[zz].astype(jnp.float32)

    half = BLK // 2
    low = lax.broadcasted_iota(jnp.int32, (1, BLK), 1) < half
    turned = pltpu.roll(total, half, 1)
    at = 0
    for pair in range(LY // 2):
        even, odd = pair * 2 * chunks, (pair * 2 + 1) * chunks
        pieces = [total[even + c : even + c + 1, :] for c in range(chunks - 1)]
        pieces.append(jnp.where(low, total[even + chunks - 1 : even + chunks, :], turned[odd : odd + 1, :]))
        for c in range(1, chunks):
            pieces.append(jnp.where(low, turned[odd + c - 1 : odd + c, :], turned[odd + c : odd + c + 1, :]))
        for piece in pieces:
            out_ref[0:1, at : at + BLK] = (piece + db_ref[0:1, at : at + BLK]).astype(jnp.bfloat16)
            at += BLK

    for n, step in enumerate(Z_STEPS):
        z_copy(z, zs, n, step).wait_send()
    for n, step in enumerate(PASSED):
        z_copy(along(step), zf, n, REACH if step < 0 else -REACH).wait_send()

    @pl.loop(1, NZ)
    def _(k):
        f_copy((z + k) % NZ, z).wait_send()

    for g in range(2):
        @pl.loop(1, NP)
        def _(k):
            p_copy(g, p, (p + k) % NP).wait_send()

        @pl.loop(1, LY)
        def _(k):
            l_copy(g, layer, (layer + k) % LY).wait_send()

        @pl.loop(1, LY * NP)
        def _(k):
            q = (mine + k) % (LY * NP)
            r_copy(g, q, mine, q).wait_send()


def shards(resid_stream, enc_mantissa, enc_exponent, enc_bias, dec_weight, dec_bias):
    width = resid_stream.shape[2]
    feats = enc_mantissa.shape[2]
    pairs, _, cols = dec_weight.shape
    blocks = width // BLK
    padded = (cols + BLK - 1) // BLK * BLK
    vm = pl.BlockSpec(memory_space=pltpu.VMEM)
    hbm = pl.BlockSpec(memory_space=pl.ANY)
    dma = pltpu.SemaphoreType.DMA
    bf, f32 = jnp.bfloat16, jnp.float32
    out = pl.pallas_call(
        kernel,
        out_shape=jax.ShapeDtypeStruct((1, width), bf),
        in_specs=[vm, hbm, vm, vm, hbm, vm],
        out_specs=vm,
        scratch_shapes=[
            pltpu.VMEM((width, feats), bf),
            pltpu.VMEM((pairs, cols, feats), bf),
            pltpu.VMEM((PITCH, BLK), f32),
            pltpu.VMEM((NZ, blocks, BLK), bf),
            pltpu.VMEM((GROUP * PITCH, BLK), f32),
            pltpu.VMEM((2, NP, GROUP, width), bf),
            pltpu.VMEM((LY, 2, NP * GROUP, feats), bf),
            pltpu.VMEM((2, LY, NP, GROUP, padded), bf),
            pltpu.VMEM((2, LY, NP, GROUP, padded), bf),
            pltpu.VMEM((GROUP * PITCH, BLK), f32),
            pltpu.VMEM((NZ, LY * padded // BLK, BLK), bf),
            pltpu.VMEM((NZ, LY * padded // BLK, BLK), bf),
            dma((2,)),
            dma((len(Z_STEPS),)), dma((len(PASSED),)), dma((NZ,)),
            dma((2, NP)), dma((2, NP)),
            dma((2, LY)), dma((2, LY)),
            dma((2, LY * NP)), dma((2, LY * NP)),
            dma((NZ,)), dma((NZ,)),
        ],
        compiler_params=pltpu.CompilerParams(collective_id=0, has_side_effects=True),
    )(
        resid_stream.reshape(1, width),
        enc_mantissa[0],
        enc_exponent.reshape(1, blocks),
        enc_bias,
        dec_weight.transpose(0, 2, 1),
        dec_bias,
    )
    return out[:, None, :]


def solution(mesh):
    in_specs = (
        P("feat", "layer", None),
        P("layer", None, "feat"),
        P("layer", None, "feat"),
        P("layer", "feat"),
        P(None, "feat", "layer"),
        P("layer", None),
    )
    out_specs = P("feat", "layer", None)
    return jax.shard_map(shards, mesh=mesh, in_specs=in_specs, out_specs=out_specs, check_vma=False)
```

time: 65.2 us -> 57 us (0.87)
  Pallas kernels: 63.7 us -> 55.4 us
    pallas_call x1, Pallas kernels: 63.7 us -> 55.4 us  [shards(): pl.pallas_call(kernel, out_shape=jax.ShapeDtypeStruct((1, width), bf), in...]
where the time goes in v3:
time: 57 us; the launch traced here: 56.7 us
  Pallas kernels  55.4 us (97%)
  local copies, waits for them, and re-layouts  1.31 us (2%)
    pallas_call x1, Pallas kernels, shards(): pl.pallas_call(kernel, out_shape=jax.ShapeDtypeStruct((1, width), bf), in...  55.4 us
    unnamed x1, local copies, waits for them, and re-layouts  1.31 us

profile of v3, /device:TPU:1, one launch (start us, length us, event | category | flops | bytes accessed | tf_op | source)
XLA Modules:
  0.0 56.7 jit_solution(6444906836474944142)
XLA Ops:
  0.0 55.4 %shard_map.64 = bf16[1,2304]{1,0:T(2,128)(2,1)} custom-call(bf16[1,2304]{1,0:T(2,128)(2,1)} %bitcast.8, bf16[2304,128]{1,0:T(8,128)(2,1)} %bitcast.6, s32[1,18]{1,0:T(1,128)} %bitcast.9, f32[1,128]{1,0:T(1,128)} %eb_ref.1, bf16[10,576,128]{2,1,0:T(8,128)(2,1)} %bitcast.5, f32[1,2304]{1,0:T(1,128)} %db_ref.1), custom_call_target="tpu_custom_call" | custom-call | tf_op jit(solution)/shard_map/pallas_call | solution.py:268
  55.4 1.3 %copy.8 = bf16[1,1,2304]{2,1,0:T(2,128)(2,1)} copy(bf16[1,1,2304]{2,1,0:T(2,128)(2,1)} %bitcast.7) | data formatting | bytes 9216

commit v4 on v3

--- a/solution.py
+++ b/solution.py
@@ -13,9 +13,7 @@
 PITCH = 24
 MESH = pl.DeviceIdType.MESH
 GROUP = 8
-REACH = 4
-Z_STEPS = (-4, 4, -3, 3, -2, 2, -1, 1)
-PASSED = (-1, 1, -2, 2, -3, 3, -4)
+Z_STEPS = (8, 7, 9, 6, 10, 5, 11, 4, 12, 3, 13, 2, 14, 1, 15)
 RING = (2, 1, 3, 0)
 PLANE = sorted(
     ((dy, dx, dc) for dy in RING for dx in RING for dc in (1, 0) if dy or dx or dc),
@@ -34,7 +32,7 @@
 def kernel(
     x_ref, m_ref, e_ref, eb_ref, d_ref, db_ref, out_ref,
     w_v, d_v, own, rows, stage, xg, lat, part, rs1, stage2, sb, rz,
-    loc_sem, zs, zf, zr, ps, pr, ls, lr, rs_s, rs_r, fs, fr,
+    loc_sem, zs, zr, ps, pr, ls, lr, rs_s, rs_r, fs, fr,
 ):
     layer = lax.axis_index("layer")
     feat = lax.axis_index("feat")
@@ -55,9 +53,6 @@
     def along(step):
         return (z + step + NZ) % NZ
 
-    def row_of(group, i):
-        return (z + NZ - REACH + GROUP * group + i) % NZ
-
     def plane_to(dy, dx, dc):
         to_y = (y + dy) % 4
         return (to_y // 2 * 2 + (core + dc) % 2) * NP + to_y % 2 * NX + (x + dx) % NX
@@ -83,14 +78,14 @@
 
     pl.semaphore_wait(barrier, len(Z_STEPS) + len(PLANE))
 
-    def z_copy(row, sems, sem, step):
-        return pltpu.make_async_remote_copy(
-            src_ref=rows.at[row], dst_ref=rows.at[row], send_sem=sems.at[sem], recv_sem=zr.at[row],
+    def z_copy(row, step):
+        return pltpu.make_async_remote_copy(
+            src_ref=rows.at[z], dst_ref=rows.at[row], send_sem=zs.at[along(step)], recv_sem=zr.at[row],
             device_id=(layer, feat_of(p, along(step))), device_id_type=MESH,
         )
 
-    for n, step in enumerate(Z_STEPS):
-        z_copy(z, zs, n, step).start()
+    for step in Z_STEPS:
+        z_copy(z, step).start()
 
     load_w.wait()
     scales = pow2(e_ref[0:1, :])
@@ -98,13 +93,6 @@
         piece = slice(b * BLK, (b + 1) * BLK)
         w_v[piece, :] = (w_v[piece, :].astype(jnp.float32) * scales[0:1, b : b + 1]).astype(jnp.bfloat16)
 
-    def arrived(step):
-        z_copy(along(step), zs, 0, 1).wait_recv()
-
-    for n, step in enumerate(PASSED):
-        arrived(step)
-        z_copy(along(step), zf, n, REACH if step < 0 else -REACH).start()
-
     def p_copy(group, slot, other):
         return pltpu.make_async_remote_copy(
             src_ref=xg.at[group, p], dst_ref=xg.at[group, slot],
@@ -114,7 +102,13 @@
 
     def spread(g):
         for i in range(GROUP):
-            stage[i * PITCH : i * PITCH + blocks, :] = rows[row_of(g, i)].astype(jnp.float32)
+            row = g * GROUP + i
+
+            @pl.when(row != z)
+            def _():
+                z_copy(row, 1).wait_recv()
+
+            stage[i * PITCH : i * PITCH + blocks, :] = rows[row].astype(jnp.float32)
         for b in range(blocks):
             xg[g, p, :, b * BLK : (b + 1) * BLK] = stage[pl.ds(b, GROUP, stride=PITCH), :].astype(jnp.bfloat16)
         for dy in (1, 0):
@@ -123,8 +117,6 @@
                     p_copy(g, p, (y_lo + dy) % 2 * NX + (x + dx) % NX).start()
 
     spread(0)
-    for step in range(REACH, REACH + GROUP):
-        arrived(step)
     spread(1)
 
     def l_copy(group, slot, other):
@@ -174,9 +166,9 @@
         rs1[g, layer, p] = part[g, layer, p]
 
     encode(0)
+    encode(1)
     load_d.wait()
     decode(0)
-    encode(1)
     decode(1)
 
     def f_copy(row, slot):
@@ -198,15 +190,18 @@
             for c in range(chunks):
                 stage2[pl.ds(s * chunks + c, GROUP, stride=PITCH), :] = total[:, c * BLK : (c + 1) * BLK]
         for i in range(GROUP):
-            sb[row_of(g, i)] = stage2[i * PITCH : i * PITCH + LY * chunks, :].astype(jnp.bfloat16)
+            sb[g * GROUP + i] = stage2[i * PITCH : i * PITCH + LY * chunks, :].astype(jnp.bfloat16)
+
+        for step in Z_STEPS:
+            row = along(step)
+
+            @pl.when(row // GROUP == g)
+            def _():
+                f_copy(row, z).start()
 
     gathered(0)
-    for step in (-4, 3, -3, 2, -2, 1, -1):
-        f_copy(along(step), z).start()
+    gathered(1)
     rz[z] = sb[z]
-    gathered(1)
-    for step in (8, 7, 9, 6, 10, 5, 11, 4):
-        f_copy(along(step), z).start()
 
     @pl.loop(1, NZ)
     def _(k):
@@ -231,13 +226,9 @@
             out_ref[0:1, at : at + BLK] = (piece + db_ref[0:1, at : at + BLK]).astype(jnp.bfloat16)
             at += BLK
 
-    for n, step in enumerate(Z_STEPS):
-        z_copy(z, zs, n, step).wait_send()
-    for n, step in enumerate(PASSED):
-        z_copy(along(step), zf, n, REACH if step < 0 else -REACH).wait_send()
-
     @pl.loop(1, NZ)
     def _(k):
+        z_copy(z, k).wait_send()
         f_copy((z + k) % NZ, z).wait_send()
 
     for g in range(2):
@@ -284,7 +275,7 @@
             pltpu.VMEM((NZ, LY * padded // BLK, BLK), bf),
             pltpu.VMEM((NZ, LY * padded // BLK, BLK), bf),
             dma((2,)),
-            dma((len(Z_STEPS),)), dma((len(PASSED),)), dma((NZ,)),
+            dma((NZ,)), dma((NZ,)),
             dma((2, NP)), dma((2, NP)),
             dma((2, LY)), dma((2, LY)),
             dma((2, LY * NP)), dma((2, LY * NP)),

time: 57 us -> 55.6 us (0.975)
  Pallas kernels: 55.4 us -> 53.7 us
    pallas_call x1, Pallas kernels: 55.4 us -> 53.7 us  [shards(): pl.pallas_call(kernel, out_shape=jax.ShapeDtypeStruct((1, width), bf), in...]
where the time goes in v4:
time: 55.6 us; the launch traced here: 55 us
  Pallas kernels  53.7 us (97%)
  local copies, waits for them, and re-layouts  1.31 us (2%)
    pallas_call x1, Pallas kernels, shards(): pl.pallas_call(kernel, out_shape=jax.ShapeDtypeStruct((1, width), bf), in...  53.7 us
    unnamed x1, local copies, waits for them, and re-layouts  1.31 us

profile of v4, /device:TPU:1, one launch (start us, length us, event | category | flops | bytes accessed | tf_op | source)
XLA Modules:
  0.0 55.0 jit_solution(11172891216017571304)
XLA Ops:
  0.0 53.7 %shard_map.64 = bf16[1,2304]{1,0:T(2,128)(2,1)} custom-call(bf16[1,2304]{1,0:T(2,128)(2,1)} %bitcast.8, bf16[2304,128]{1,0:T(8,128)(2,1)} %bitcast.6, s32[1,18]{1,0:T(1,128)} %bitcast.9, f32[1,128]{1,0:T(1,128)} %eb_ref.1, bf16[10,576,128]{2,1,0:T(8,128)(2,1)} %bitcast.5, f32[1,2304]{1,0:T(1,128)} %db_ref.1), custom_call_target="tpu_custom_call" | custom-call | tf_op jit(solution)/shard_map/pallas_call | solution.py:259
  53.7 1.3 %copy.8 = bf16[1,1,2304]{2,1,0:T(2,128)(2,1)} copy(bf16[1,1,2304]{2,1,0:T(2,128)(2,1)} %bitcast.7) | data formatting | bytes 9216

commit v5 on v4

--- a/solution.py
+++ b/solution.py
@@ -12,9 +12,12 @@
 BLK = 128
 PITCH = 24
 MESH = pl.DeviceIdType.MESH
-GROUP = 8
+SIZES = (4, 4, 8)
+STARTS = tuple(sum(SIZES[:n]) for n in range(len(SIZES)))
+GROUPS = range(len(SIZES))
 Z_STEPS = (8, 7, 9, 6, 10, 5, 11, 4, 12, 3, 13, 2, 14, 1, 15)
 RING = (2, 1, 3, 0)
+CROSS = [(2, 0, 0), (0, 2, 0), (1, 0, 0), (3, 0, 0), (0, 1, 0), (0, 3, 0), (0, 0, 1)]
 PLANE = sorted(
     ((dy, dx, dc) for dy in RING for dx in RING for dc in (1, 0) if dy or dx or dc),
     key=lambda s: -(min(s[0], 4 - s[0]) + min(s[1], 4 - s[1])),
@@ -30,9 +33,9 @@
 
 
 def kernel(
-    x_ref, m_ref, e_ref, eb_ref, d_ref, db_ref, out_ref,
-    w_v, d_v, own, rows, stage, xg, lat, part, rs1, stage2, sb, rz,
-    loc_sem, zs, zr, ps, pr, ls, lr, rs_s, rs_r, fs, fr,
+    x_in, m_ref, e_in, eb_in, d_ref, db_in, out_ref,
+    x_ref, e_ref, eb_ref, db_ref, w_v, d_v, own, rows, stage, xgs, lat, parts, rs1s, stage2, sb, rz,
+    loc_sem, ready, zs, zr, ps, pr, ls, lr, rs_s, rs_r, fs, fr,
 ):
     layer = lax.axis_index("layer")
     feat = lax.axis_index("feat")
@@ -42,13 +45,16 @@
     p = y_lo * NX + x
     y, core = layer // 2 * 2 + y_lo, layer % 2
     mine = layer * NP + p
-    width = x_ref.shape[1]
+    width = x_in.shape[1]
     blocks = width // BLK
     cols = d_ref.shape[1]
-    chunks = part.shape[4] // BLK
+    chunks = parts[0].shape[3] // BLK
 
     def feat_of(place, zz):
         return (place // NX) * (NZ * NX) + zz * NX + place % NX
+
+    def rows_of(group):
+        return slice(STARTS[group] * NP, (STARTS[group] + SIZES[group]) * NP)
 
     def along(step):
         return (z + step + NZ) % NZ
@@ -57,26 +63,33 @@
         to_y = (y + dy) % 4
         return (to_y // 2 * 2 + (core + dc) % 2) * NP + to_y % 2 * NX + (x + dx) % NX
 
+    small = [
+        pltpu.make_async_copy(src, dst, loc_sem.at[2 + n])
+        for n, (src, dst) in enumerate(((x_in, x_ref), (e_in, e_ref), (eb_in, eb_ref), (db_in, db_ref)))
+    ]
     load_w = pltpu.make_async_copy(m_ref, w_v, loc_sem.at[0])
     load_d = pltpu.make_async_copy(d_ref, d_v, loc_sem.at[1])
-    load_w.start()
-    load_d.start()
 
     barrier = pltpu.get_barrier_semaphore()
     for step in Z_STEPS:
         pl.semaphore_signal(barrier, inc=1, device_id=(layer, feat_of(p, along(step))), device_id_type=MESH)
-    for dy, dx, dc in PLANE:
+    for dy, dx, dc in CROSS:
         to = plane_to(dy, dx, dc)
         pl.semaphore_signal(barrier, inc=1, device_id=(to // NP, feat_of(to % NP, z)), device_id_type=MESH)
+    for copy in small:
+        copy.start()
+    load_w.start()
+    load_d.start()
+    small[0].wait()
 
     for b in range(blocks):
         own[b : b + 1, :] = x_ref[0:1, b * BLK : (b + 1) * BLK].astype(jnp.float32)
     rows[z] = own[0:blocks, :].astype(jnp.bfloat16)
-    for g in range(2):
+    for g in GROUPS:
         for t in range(LY):
-            part[g, t, :, :, 512:640] = jnp.zeros((NP, GROUP, 128), jnp.bfloat16)
-
-    pl.semaphore_wait(barrier, len(Z_STEPS) + len(PLANE))
+            parts[g][t, :, :, 512:640] = jnp.zeros((NP, SIZES[g], 128), jnp.bfloat16)
+
+    pl.semaphore_wait(barrier, len(Z_STEPS) + len(CROSS))
 
     def z_copy(row, step):
         return pltpu.make_async_remote_copy(
@@ -87,22 +100,32 @@
     for step in Z_STEPS:
         z_copy(z, step).start()
 
+    for dx in RING[:3]:
+        to = plane_to(0, dx, 0)
+        pl.semaphore_signal(ready.at[0], inc=1, device_id=(to // NP, feat_of(to % NP, z)), device_id_type=MESH)
+
+    for copy in small[1:]:
+        copy.wait()
     load_w.wait()
     scales = pow2(e_ref[0:1, :])
     for b in range(blocks):
         piece = slice(b * BLK, (b + 1) * BLK)
         w_v[piece, :] = (w_v[piece, :].astype(jnp.float32) * scales[0:1, b : b + 1]).astype(jnp.bfloat16)
 
+    pl.semaphore_wait(ready.at[0], NX - 1)
+    to = plane_to(0, 0, 1)
+    pl.semaphore_signal(ready.at[1], inc=1, device_id=(to // NP, feat), device_id_type=MESH)
+
     def p_copy(group, slot, other):
         return pltpu.make_async_remote_copy(
-            src_ref=xg.at[group, p], dst_ref=xg.at[group, slot],
+            src_ref=xgs[group].at[p], dst_ref=xgs[group].at[slot],
             send_sem=ps.at[group, other], recv_sem=pr.at[group, slot],
             device_id=(layer, feat_of(other, z)), device_id_type=MESH,
         )
 
     def spread(g):
-        for i in range(GROUP):
-            row = g * GROUP + i
+        for i in range(SIZES[g]):
+            row = STARTS[g] + i
 
             @pl.when(row != z)
             def _():
@@ -110,23 +133,22 @@
 
             stage[i * PITCH : i * PITCH + blocks, :] = rows[row].astype(jnp.float32)
         for b in range(blocks):
-            xg[g, p, :, b * BLK : (b + 1) * BLK] = stage[pl.ds(b, GROUP, stride=PITCH), :].astype(jnp.bfloat16)
+            xgs[g][p, :, b * BLK : (b + 1) * BLK] = stage[pl.ds(b, SIZES[g], stride=PITCH), :].astype(jnp.bfloat16)
         for dy in (1, 0):
             for dx in RING:
                 if dy or dx:
                     p_copy(g, p, (y_lo + dy) % 2 * NX + (x + dx) % NX).start()
 
-    spread(0)
-    spread(1)
+    for g in GROUPS:
+        spread(g)
 
     def l_copy(group, slot, other):
         return pltpu.make_async_remote_copy(
-            src_ref=lat.at[layer, group], dst_ref=lat.at[slot, group],
+            src_ref=lat.at[layer, rows_of(group)], dst_ref=lat.at[slot, rows_of(group)],
             send_sem=ls.at[group, other], recv_sem=lr.at[group, slot],
             device_id=(other, feat), device_id_type=MESH,
         )
 
-    tokens = NP * GROUP
 
     def encode(g):
         @pl.loop(1, NP)
@@ -134,14 +156,14 @@
             other = (p + k) % NP
             p_copy(g, other, other).wait_recv()
 
-        pre = jnp.dot(xg[g].reshape(tokens, width), w_v[...], preferred_element_type=jnp.float32)
-        lat[layer, g] = jnp.maximum(pre + eb_ref[...], 0.0).astype(jnp.bfloat16)
+        pre = jnp.dot(xgs[g][...].reshape(NP * SIZES[g], width), w_v[...], preferred_element_type=jnp.float32)
+        lat[layer, rows_of(g)] = jnp.maximum(pre + eb_ref[...], 0.0).astype(jnp.bfloat16)
         for k in (2, 3, 1):
             l_copy(g, layer, (layer + k) % LY).start()
 
     def r_copy(group, src, slot, other):
         return pltpu.make_async_remote_copy(
-            src_ref=part.at[group, src // NP, src % NP], dst_ref=rs1.at[group, slot // NP, slot % NP],
+            src_ref=parts[group].at[src // NP, src % NP], dst_ref=rs1s[group].at[slot // NP, slot % NP],
             send_sem=rs_s.at[group, other], recv_sem=rs_r.at[group, slot],
             device_id=(other // NP, feat_of(other % NP, z)), device_id_type=MESH,
         )
@@ -153,23 +175,24 @@
             l_copy(g, other, other).wait_recv()
 
         for t in range(LY):
-            total = jnp.zeros((tokens, cols), jnp.float32)
+            total = jnp.zeros((NP * SIZES[g], cols), jnp.float32)
             for s in range(t + 1):
                 total = total + lax.dot_general(
-                    lat[s, g], d_v[t * (t + 1) // 2 + s], (((1,), (1,)), ((), ())),
+                    lat[s, rows_of(g)], d_v[t * (t + 1) // 2 + s], (((1,), (1,)), ((), ())),
                     preferred_element_type=jnp.float32,
                 )
-            part[g, t, :, :, 0:cols] = total.reshape(NP, GROUP, cols).astype(jnp.bfloat16)
+            parts[g][t, :, :, 0:cols] = total.reshape(NP, SIZES[g], cols).astype(jnp.bfloat16)
         for dy, dx, dc in PLANE:
             to = plane_to(dy, dx, dc)
             r_copy(g, to, mine, to).start()
-        rs1[g, layer, p] = part[g, layer, p]
-
-    encode(0)
-    encode(1)
+        rs1s[g][layer, p] = parts[g][layer, p]
+
+    pl.semaphore_wait(ready.at[1], 1)
+    for g in GROUPS:
+        encode(g)
     load_d.wait()
-    decode(0)
-    decode(1)
+    for g in GROUPS:
+        decode(g)
 
     def f_copy(row, slot):
         return pltpu.make_async_remote_copy(
@@ -184,23 +207,23 @@
             r_copy(g, q, q, q).wait_recv()
 
         for s in range(LY):
-            total = rs1[g, s, 0].astype(jnp.float32)
+            total = rs1s[g][s, 0].astype(jnp.float32)
             for place in range(1, NP):
-                total = total + rs1[g, s, place].astype(jnp.float32)
+                total = total + rs1s[g][s, place].astype(jnp.float32)
             for c in range(chunks):
-                stage2[pl.ds(s * chunks + c, GROUP, stride=PITCH), :] = total[:, c * BLK : (c + 1) * BLK]
-        for i in range(GROUP):
-            sb[g * GROUP + i] = stage2[i * PITCH : i * PITCH + LY * chunks, :].astype(jnp.bfloat16)
+                stage2[pl.ds(s * chunks + c, SIZES[g], stride=PITCH), :] = total[:, c * BLK : (c + 1) * BLK]
+        for i in range(SIZES[g]):
+            sb[STARTS[g] + i] = stage2[i * PITCH : i * PITCH + LY * chunks, :].astype(jnp.bfloat16)
 
         for step in Z_STEPS:
             row = along(step)
 
-            @pl.when(row // GROUP == g)
+            @pl.when((row >= STARTS[g]) & (row < STARTS[g] + SIZES[g]))
             def _():
                 f_copy(row, z).start()
 
-    gathered(0)
-    gathered(1)
+    for g in GROUPS:
+        gathered(g)
     rz[z] = sb[z]
 
     @pl.loop(1, NZ)
@@ -231,7 +254,7 @@
         z_copy(z, k).wait_send()
         f_copy((z + k) % NZ, z).wait_send()
 
-    for g in range(2):
+    for g in GROUPS:
         @pl.loop(1, NP)
         def _(k):
             p_copy(g, p, (p + k) % NP).wait_send()
@@ -259,26 +282,31 @@
     out = pl.pallas_call(
         kernel,
         out_shape=jax.ShapeDtypeStruct((1, width), bf),
-        in_specs=[vm, hbm, vm, vm, hbm, vm],
+        in_specs=[hbm] * 6,
         out_specs=vm,
         scratch_shapes=[
+            pltpu.VMEM((1, width), bf),
+            pltpu.VMEM((1, blocks), jnp.int32),
+            pltpu.VMEM((1, feats), f32),
+            pltpu.VMEM((1, width), f32),
             pltpu.VMEM((width, feats), bf),
             pltpu.VMEM((pairs, cols, feats), bf),
             pltpu.VMEM((PITCH, BLK), f32),
             pltpu.VMEM((NZ, blocks, BLK), bf),
-            pltpu.VMEM((GROUP * PITCH, BLK), f32),
-            pltpu.VMEM((2, NP, GROUP, width), bf),
-            pltpu.VMEM((LY, 2, NP * GROUP, feats), bf),
-            pltpu.VMEM((2, LY, NP, GROUP, padded), bf),
-            pltpu.VMEM((2, LY, NP, GROUP, padded), bf),
-            pltpu.VMEM((GROUP * PITCH, BLK), f32),
+            pltpu.VMEM((max(SIZES) * PITCH, BLK), f32),
+            [pltpu.VMEM((NP, size, width), bf) for size in SIZES],
+            pltpu.VMEM((LY, NP * NZ, feats), bf),
+            [pltpu.VMEM((LY, NP, size, padded), bf) for size in SIZES],
+            [pltpu.VMEM((LY, NP, size, padded), bf) for size in SIZES],
+            pltpu.VMEM((max(SIZES) * PITCH, BLK), f32),
             pltpu.VMEM((NZ, LY * padded // BLK, BLK), bf),
             pltpu.VMEM((NZ, LY * padded // BLK, BLK), bf),
-            dma((2,)),
+            dma((6,)),
+            pltpu.SemaphoreType.REGULAR((2,)),
             dma((NZ,)), dma((NZ,)),
-            dma((2, NP)), dma((2, NP)),
-            dma((2, LY)), dma((2, LY)),
-            dma((2, LY * NP)), dma((2, LY * NP)),
+            dma((len(SIZES), NP)), dma((len(SIZES), NP)),
+            dma((len(SIZES), LY)), dma((len(SIZES), LY)),
+            dma((len(SIZES), LY * NP)), dma((len(SIZES), LY * NP)),
             dma((NZ,)), dma((NZ,)),
         ],
         compiler_params=pltpu.CompilerParams(collective_id=0, has_side_effects=True),

time: 55.6 us -> 54.1 us (0.973)
  the two profiles are of different devices: /device:TPU:1 before, /device:TPU:4 now
where the time goes in v5:
time: 54.1 us; the launch traced here: 53.8 us
  Pallas kernels  52.5 us (97%)
  local copies, waits for them, and re-layouts  1.31 us (2%)
    pallas_call x1, Pallas kernels, shards(): pl.pallas_call(kernel, out_shape=jax.ShapeDtypeStruct((1, width), bf), in...  52.5 us
    unnamed x1, local copies, waits for them, and re-layouts  1.31 us

profile of v5, /device:TPU:4, one launch (start us, length us, event | category | flops | bytes accessed | tf_op | source)
XLA Modules:
  0.0 53.8 jit_solution(1435238862189634024)
XLA Ops:
  0.0 52.5 %shard_map.64 = bf16[1,2304]{1,0:T(2,128)(2,1)} custom-call(bf16[1,2304]{1,0:T(2,128)(2,1)} %bitcast.8, bf16[2304,128]{1,0:T(8,128)(2,1)} %bitcast.6, s32[1,18]{1,0:T(1,128)} %bitcast.9, f32[1,128]{1,0:T(1,128)} %eb_in.1, bf16[10,576,128]{2,1,0:T(8,128)(2,1)} %bitcast.5, f32[1,2304]{1,0:T(1,128)} %db_in.1), custom_call_target="tpu_custom_call" | custom-call | tf_op jit(solution)/shard_map/pallas_call | solution.py:282
  52.5 1.3 %copy.8 = bf16[1,1,2304]{2,1,0:T(2,128)(2,1)} copy(bf16[1,1,2304]{2,1,0:T(2,128)(2,1)} %bitcast.7) | data formatting | bytes 9216

commit v6 on v5

--- a/solution.py
+++ b/solution.py
@@ -39,29 +39,35 @@
 ):
     layer = lax.axis_index("layer")
     feat = lax.axis_index("feat")
-    y_lo = feat // (NZ * NX)
-    z = (feat // NX) % NZ
-    x = feat % NX
+    y_hi = jnp.where(layer >= 2, 1, 0)
+    core = layer - 2 * y_hi
+    y_lo = jnp.where(feat >= NZ * NX, 1, 0)
+    z = lax.div(feat - y_lo * (NZ * NX), NX)
+    x = feat - y_lo * (NZ * NX) - z * NX
     p = y_lo * NX + x
-    y, core = layer // 2 * 2 + y_lo, layer % 2
-    mine = layer * NP + p
+    y = 2 * y_hi + y_lo
     width = x_in.shape[1]
     blocks = width // BLK
     cols = d_ref.shape[1]
     chunks = parts[0].shape[3] // BLK
 
     def feat_of(place, zz):
-        return (place // NX) * (NZ * NX) + zz * NX + place % NX
+        return place + jnp.where(place >= NX, NZ * NX - NX, 0) + zz * NX
+
+    def wrap(value, length):
+        return jnp.where(value >= length, value - length, value)
 
     def rows_of(group):
         return slice(STARTS[group] * NP, (STARTS[group] + SIZES[group]) * NP)
 
     def along(step):
-        return (z + step + NZ) % NZ
+        return wrap(z + step, NZ)
 
     def plane_to(dy, dx, dc):
-        to_y = (y + dy) % 4
-        return (to_y // 2 * 2 + (core + dc) % 2) * NP + to_y % 2 * NX + (x + dx) % NX
+        to_y = wrap(y + dy, 4)
+        to_core = 1 - core if dc else core
+        to_lo = 1 - y_lo if dy % 2 else y_lo
+        return jnp.where(to_y >= 2, 2, 0) + to_core, to_lo * NX + wrap(x + dx, NX)
 
     small = [
         pltpu.make_async_copy(src, dst, loc_sem.at[2 + n])
@@ -75,7 +81,7 @@
         pl.semaphore_signal(barrier, inc=1, device_id=(layer, feat_of(p, along(step))), device_id_type=MESH)
     for dy, dx, dc in CROSS:
         to = plane_to(dy, dx, dc)
-        pl.semaphore_signal(barrier, inc=1, device_id=(to // NP, feat_of(to % NP, z)), device_id_type=MESH)
+        pl.semaphore_signal(barrier, inc=1, device_id=(to[0], feat_of(to[1], z)), device_id_type=MESH)
     for copy in small:
         copy.start()
     load_w.start()
@@ -102,7 +108,7 @@
 
     for dx in RING[:3]:
         to = plane_to(0, dx, 0)
-        pl.semaphore_signal(ready.at[0], inc=1, device_id=(to // NP, feat_of(to % NP, z)), device_id_type=MESH)
+        pl.semaphore_signal(ready.at[0], inc=1, device_id=(to[0], feat_of(to[1], z)), device_id_type=MESH)
 
     for copy in small[1:]:
         copy.wait()
@@ -114,7 +120,7 @@
 
     pl.semaphore_wait(ready.at[0], NX - 1)
     to = plane_to(0, 0, 1)
-    pl.semaphore_signal(ready.at[1], inc=1, device_id=(to // NP, feat), device_id_type=MESH)
+    pl.semaphore_signal(ready.at[1], inc=1, device_id=(to[0], feat), device_id_type=MESH)
 
     def p_copy(group, slot, other):
         return pltpu.make_async_remote_copy(
@@ -137,7 +143,7 @@
         for dy in (1, 0):
             for dx in RING:
                 if dy or dx:
-                    p_copy(g, p, (y_lo + dy) % 2 * NX + (x + dx) % NX).start()
+                    p_copy(g, p, plane_to(dy, dx, 0)[1]).start()
 
     for g in GROUPS:
         spread(g)
@@ -153,25 +159,26 @@
     def encode(g):
         @pl.loop(1, NP)
         def _(k):
-            other = (p + k) % NP
+            other = wrap(p + k, NP)
             p_copy(g, other, other).wait_recv()
 
         pre = jnp.dot(xgs[g][...].reshape(NP * SIZES[g], width), w_v[...], preferred_element_type=jnp.float32)
         lat[layer, rows_of(g)] = jnp.maximum(pre + eb_ref[...], 0.0).astype(jnp.bfloat16)
         for k in (2, 3, 1):
-            l_copy(g, layer, (layer + k) % LY).start()
-
-    def r_copy(group, src, slot, other):
-        return pltpu.make_async_remote_copy(
-            src_ref=parts[group].at[src // NP, src % NP], dst_ref=rs1s[group].at[slot // NP, slot % NP],
-            send_sem=rs_s.at[group, other], recv_sem=rs_r.at[group, slot],
-            device_id=(other // NP, feat_of(other % NP, z)), device_id_type=MESH,
+            l_copy(g, layer, wrap(layer + k, LY)).start()
+
+    def r_copy(group, n):
+        to = plane_to(*PLANE[n])
+        return pltpu.make_async_remote_copy(
+            src_ref=parts[group].at[to[0], to[1]], dst_ref=rs1s[group].at[layer, p],
+            send_sem=rs_s.at[group, n], recv_sem=rs_r.at[group, n],
+            device_id=(to[0], feat_of(to[1], z)), device_id_type=MESH,
         )
 
     def decode(g):
         @pl.loop(1, LY)
         def _(k):
-            other = (layer + k) % LY
+            other = wrap(layer + k, LY)
             l_copy(g, other, other).wait_recv()
 
         for t in range(LY):
@@ -182,9 +189,8 @@
                     preferred_element_type=jnp.float32,
                 )
             parts[g][t, :, :, 0:cols] = total.reshape(NP, SIZES[g], cols).astype(jnp.bfloat16)
-        for dy, dx, dc in PLANE:
-            to = plane_to(dy, dx, dc)
-            r_copy(g, to, mine, to).start()
+        for n in range(len(PLANE)):
+            r_copy(g, n).start()
         rs1s[g][layer, p] = parts[g][layer, p]
 
     pl.semaphore_wait(ready.at[1], 1)
@@ -201,10 +207,8 @@
         )
 
     def gathered(g):
-        @pl.loop(1, LY * NP)
-        def _(k):
-            q = (mine + k) % (LY * NP)
-            r_copy(g, q, q, q).wait_recv()
+        for n in range(len(PLANE)):
+            r_copy(g, n).wait_recv()
 
         for s in range(LY):
             total = rs1s[g][s, 0].astype(jnp.float32)
@@ -228,7 +232,7 @@
 
     @pl.loop(1, NZ)
     def _(k):
-        other = (z + k) % NZ
+        other = wrap(z + k, NZ)
         f_copy(other, other).wait_recv()
 
     total = rz[0].astype(jnp.float32)
@@ -252,21 +256,19 @@
     @pl.loop(1, NZ)
     def _(k):
         z_copy(z, k).wait_send()
-        f_copy((z + k) % NZ, z).wait_send()
+        f_copy(wrap(z + k, NZ), z).wait_send()
 
     for g in GROUPS:
         @pl.loop(1, NP)
         def _(k):
-            p_copy(g, p, (p + k) % NP).wait_send()
+            p_copy(g, p, wrap(p + k, NP)).wait_send()
 
         @pl.loop(1, LY)
         def _(k):
-            l_copy(g, layer, (layer + k) % LY).wait_send()
-
-        @pl.loop(1, LY * NP)
-        def _(k):
-            q = (mine + k) % (LY * NP)
-            r_copy(g, q, mine, q).wait_send()
+            l_copy(g, layer, wrap(layer + k, LY)).wait_send()
+
+        for n in range(len(PLANE)):
+            r_copy(g, n).wait_send()
 
 
 def shards(resid_stream, enc_mantissa, enc_exponent, enc_bias, dec_weight, dec_bias):

time: 54.1 us -> 51.3 us (0.948)
  the two profiles are of different devices: /device:TPU:4 before, /device:TPU:1 now
where the time goes in v6:
time: 51.3 us; the launch traced here: 51.1 us
  Pallas kernels  49.8 us (97%)
  local copies, waits for them, and re-layouts  1.31 us (3%)
    pallas_call x1, Pallas kernels, shards(): pl.pallas_call(kernel, out_shape=jax.ShapeDtypeStruct((1, width), bf), in...  49.8 us
    unnamed x1, local copies, waits for them, and re-layouts  1.31 us

profile of v6, /device:TPU:1, one launch (start us, length us, event | category | flops | bytes accessed | tf_op | source)
XLA Modules:
  0.0 51.1 jit_solution(8551464779478868822)
XLA Ops:
  0.0 49.8 %shard_map.64 = bf16[1,2304]{1,0:T(2,128)(2,1)} custom-call(bf16[1,2304]{1,0:T(2,128)(2,1)} %bitcast.8, bf16[2304,128]{1,0:T(8,128)(2,1)} %bitcast.6, s32[1,18]{1,0:T(1,128)} %bitcast.9, f32[1,128]{1,0:T(1,128)} %eb_in.1, bf16[10,576,128]{2,1,0:T(8,128)(2,1)} %bitcast.5, f32[1,2304]{1,0:T(1,128)} %db_in.1), custom_call_target="tpu_custom_call" | custom-call | tf_op jit(solution)/shard_map/pallas_call | solution.py:284
  49.8 1.3 %copy.8 = bf16[1,1,2304]{2,1,0:T(2,128)(2,1)} copy(bf16[1,1,2304]{2,1,0:T(2,128)(2,1)} %bitcast.7) | data formatting | bytes 9216

commit v7 on v6

--- a/solution.py
+++ b/solution.py
@@ -182,12 +182,12 @@
             l_copy(g, other, other).wait_recv()
 
         for t in range(LY):
-            total = jnp.zeros((NP * SIZES[g], cols), jnp.float32)
-            for s in range(t + 1):
-                total = total + lax.dot_general(
-                    lat[s, rows_of(g)], d_v[t * (t + 1) // 2 + s], (((1,), (1,)), ((), ())),
-                    preferred_element_type=jnp.float32,
-                )
+            first = t * (t + 1) // 2
+            total = lax.dot_general(
+                jnp.concatenate([lat[s, rows_of(g)] for s in range(t + 1)], axis=1),
+                jnp.concatenate([d_v[first + s] for s in range(t + 1)], axis=1),
+                (((1,), (1,)), ((), ())), preferred_element_type=jnp.float32,
+            )
             parts[g][t, :, :, 0:cols] = total.reshape(NP, SIZES[g], cols).astype(jnp.bfloat16)
         for n in range(len(PLANE)):
             r_copy(g, n).start()
@@ -219,10 +219,9 @@
         for i in range(SIZES[g]):
             sb[STARTS[g] + i] = stage2[i * PITCH : i * PITCH + LY * chunks, :].astype(jnp.bfloat16)
 
-        for step in Z_STEPS:
-            row = along(step)
-
-            @pl.when((row >= STARTS[g]) & (row < STARTS[g] + SIZES[g]))
+        for row in range(STARTS[g], STARTS[g] + SIZES[g]):
+
+            @pl.when(row != z)
             def _():
                 f_copy(row, z).start()
 

time: 51.3 us -> 51.7 us (level)
  no operation moved by 1% of the time
where the time goes in v7:
time: 51.7 us; the launch traced here: 51.1 us
  Pallas kernels  49.8 us (96%)
  local copies, waits for them, and re-layouts  1.31 us (3%)
    pallas_call x1, Pallas kernels, shards(): pl.pallas_call(kernel, out_shape=jax.ShapeDtypeStruct((1, width), bf), in...  49.8 us
    unnamed x1, local copies, waits for them, and re-layouts  1.31 us

profile of v7, /device:TPU:1, one launch (start us, length us, event | category | flops | bytes accessed | tf_op | source)
XLA Modules:
  0.0 51.1 jit_solution(6136247873921460245)
XLA Ops:
  0.0 49.8 %shard_map.64 = bf16[1,2304]{1,0:T(2,128)(2,1)} custom-call(bf16[1,2304]{1,0:T(2,128)(2,1)} %bitcast.8, bf16[2304,128]{1,0:T(8,128)(2,1)} %bitcast.6, s32[1,18]{1,0:T(1,128)} %bitcast.9, f32[1,128]{1,0:T(1,128)} %eb_in.1, bf16[10,576,128]{2,1,0:T(8,128)(2,1)} %bitcast.5, f32[1,2304]{1,0:T(1,128)} %db_in.1), custom_call_target="tpu_custom_call" | custom-call | tf_op jit(solution)/shard_map/pallas_call | solution.py:283
  49.8 1.3 %copy.8 = bf16[1,1,2304]{2,1,0:T(2,128)(2,1)} copy(bf16[1,1,2304]{2,1,0:T(2,128)(2,1)} %bitcast.7) | data formatting | bytes 9216
